TPU v7x, 32 devices: a whole 2x2x4 slice. The times are simulated.
32 devices in a mesh: head: 4 (over z), tok: 8 (over y, x, core).
Axes of the slice: x: 2, y: 2, z: 4, core: 2. Of those that a mesh axis runs over, the one named last changes fastest.
Arguments:
- video_q: bfloat16 [7168, 2048], P('tok', 'head'), may hold values from -6 to 6
- video_k: bfloat16 [7168, 2048], P('tok', 'head'), may hold values from -6 to 6
- video_v: bfloat16 [7168, 2048], P('tok', 'head'), may hold values from -6 to 6
- audio_q: bfloat16 [256, 2048], P('tok', 'head'), may hold values from -6 to 6
- audio_k: bfloat16 [256, 2048], P('tok', 'head'), may hold values from -6 to 6
- audio_v: bfloat16 [256, 2048], P('tok', 'head'), may hold values from -6 to 6
- norm_gain: float32 [2048], replicated, may hold values from 0.5 to 1.5
Outputs:
- video_out: bfloat16 [7168, 2048], P(('tok', 'head'))
- audio_out: bfloat16 [256, 2048], P('tok', 'head')
All inputs are finite; a program needn't handle non-finite values.
Results may differ from a plain program's by a relative error of at most 0.0095.
Values may be sent and summed in bfloat16 or wider, within the bound.
No kernel may reach another device: no remote copies, remote signals or barrier semaphores. Data moves between devices by JAX's collectives and lax.ppermute only.
A program may use at most 64 MiB of HBM per device.

v0:
```python
import jax
import jax.numpy as jnp
from jax import lax
from jax.sharding import PartitionSpec as P

HEAD_DIM = 64


def shards(video_q, video_k, video_v, audio_q, audio_k, audio_v, norm_gain):
    query_rows, local_width = video_q.shape
    heads_here = local_width // HEAD_DIM
    audio_rows = audio_q.shape[0]
    scaling = HEAD_DIM ** (-0.5)

    def split_heads(matrix):
        return matrix.reshape(matrix.shape[0], heads_here, HEAD_DIM)

    video_heads = split_heads(video_q)
    pieces = (
        lax.all_gather(audio_k, "tok", axis=0, tiled=True),
        lax.all_gather(audio_v, "tok", axis=0, tiled=True),
    )
    running_max = jnp.full((heads_here, query_rows), -1e30, jnp.float32)
    running_sum = jnp.zeros((heads_here, query_rows), jnp.float32)
    running_out = jnp.zeros((heads_here, query_rows, HEAD_DIM), jnp.float32)
    key_block = split_heads(pieces[0])
    value_block = split_heads(pieces[1])
    max_list = []
    sum_list = []
    out_list = []
    for absorb_head_index in range(heads_here):
        absorb_scores = (
            jnp.einsum(
                "qd,kd->qk",
                video_heads[:, absorb_head_index],
                key_block[:, absorb_head_index],
                preferred_element_type=jnp.float32,
            )
            * scaling
        )
        new_max = jnp.maximum(running_max[absorb_head_index], jnp.max(absorb_scores, axis=1))
        absorb_weights = jnp.exp(absorb_scores - new_max[:, None])
        factor = jnp.exp(running_max[absorb_head_index] - new_max)
        sum_list.append(running_sum[absorb_head_index] * factor + jnp.sum(absorb_weights, axis=1))
        out_list.append(
            running_out[absorb_head_index] * factor[:, None]
            + jnp.dot(
                absorb_weights.astype(jnp.bfloat16),
                value_block[:, absorb_head_index],
                preferred_element_type=jnp.float32,
            )
        )
        max_list.append(new_max)
    final_sum = jnp.stack(sum_list)
    final_out = jnp.stack(out_list)
    video_attn = (
        (final_out / final_sum[:, :, None]).transpose(1, 0, 2).reshape(query_rows, local_width)
    )
    video_attn = video_attn.astype(jnp.bfloat16)
    head_count = lax.axis_size("head")
    pieces = video_attn.reshape(head_count, query_rows // head_count, local_width)
    received = lax.all_to_all(pieces, "head", split_axis=0, concat_axis=2, tiled=True)
    normalize_received = received[0]
    widened = normalize_received.astype(jnp.float32)
    mean_square = jnp.mean(widened * widened, axis=-1, keepdims=True)
    video_out = (widened * lax.rsqrt(mean_square + 1e-06) * norm_gain).astype(jnp.bfloat16)
    all_queries = split_heads(lax.all_gather(audio_q, "tok", axis=0, tiled=True))
    video_keys = split_heads(video_k)
    video_values = split_heads(video_v)
    max_list, sum_list, out_list = ([], [], [])
    for head_index in range(heads_here):
        scores = (
            jnp.einsum(
                "qd,kd->qk",
                all_queries[:, head_index],
                video_keys[:, head_index],
                preferred_element_type=jnp.float32,
            )
            * scaling
        )
        local_max = jnp.max(scores, axis=1)
        weights = jnp.exp(scores - local_max[:, None])
        max_list.append(local_max)
        sum_list.append(jnp.sum(weights, axis=1))
        out_list.append(
            jnp.dot(
                weights.astype(jnp.bfloat16),
                video_values[:, head_index],
                preferred_element_type=jnp.float32,
            )
        )
    part_max = jnp.stack(max_list)
    part_sum = jnp.stack(sum_list)
    part_out = jnp.stack(out_list)
    tok_count = lax.axis_size("tok")
    grouped_max = part_max.reshape(heads_here, tok_count, audio_rows)
    grouped_sum = part_sum.reshape(heads_here, tok_count, audio_rows)
    grouped_out = part_out.reshape(heads_here, tok_count, audio_rows, HEAD_DIM)
    got_max, got_sum, got_out = (
        lax.all_to_all(grouped_max, "tok", split_axis=1, concat_axis=1, tiled=True),
        lax.all_to_all(grouped_sum, "tok", split_axis=1, concat_axis=1, tiled=True),
        lax.all_to_all(grouped_out, "tok", split_axis=1, concat_axis=1, tiled=True),
    )
    joint_max = jnp.max(got_max, axis=1, keepdims=True)
    factor = jnp.exp(got_max - joint_max)
    own_sum = jnp.sum(got_sum * factor, axis=1)
    own_out = jnp.sum(got_out * factor[:, :, :, None], axis=1)
    audio_out = (own_out / own_sum[:, :, None]).transpose(1, 0, 2).reshape(audio_rows, local_width)
    return (video_out, audio_out.astype(jnp.bfloat16))


def solution(mesh):
    placed = (
        P("tok", "head"),
        P("tok", "head"),
        P("tok", "head"),
        P("tok", "head"),
        P("tok", "head"),
        P("tok", "head"),
        P(),
    )
    return jax.shard_map(
        shards,
        mesh=mesh,
        in_specs=placed,
        out_specs=(P(("tok", "head"), None), P("tok", "head")),
        check_vma=False,
    )
```

profile of v0, /device:TPU:2, one launch (start us, length us, event | category | flops | bytes accessed | tf_op | source)
XLA Modules:
  0.0 136.5 jit_solution(5439281923956498559)
XLA Ops:
  0.6 1.5 %copy.41 = bf16[896,512]{0,1:T(8,128)(2,1)S(1)} copy(bf16[896,512]{1,0:T(8,128)(2,1)} %param.8) | data formatting | bytes 1835008 | tf_op args[1]
  2.2 9.3 %all_gather.11 = bf16[256,512]{1,0:T(8,128)(2,1)S(1)} all-gather(bf16[32,512]{1,0:T(8,128)(2,1)S(1)} %copy-done.27), channel_id=1, replica_groups=mesh['head'=4,'tok'=8] {'tok'}, dimensions={0}, use_global_device_ids=true | all-gather | bytes 294912 | tf_op jit(solution)/shard_map/all_gather | solution.py:67
  11.6 1.3 fusion.91
  12.9 1.2 fusion.92
  14.2 1.3 fusion.93
  15.5 1.2 fusion.94
  16.7 1.3 fusion.95
  18.0 1.3 fusion.96
  19.2 1.2 fusion.97
  20.5 1.2 fusion.98
  22.5 0.7 reshape.485
  23.2 3.8 %all-to-all-start.2 = ((f32[8,1,256]{2,1,0:T(1,128)}), f32[8,1,256]{2,1,0:T(1,128)S(1)}, u32[]{:S(2)}, u32[]{:S(2)}) async-start(f32[8,1,256]{2,1,0:T(1,128)} %reshape.485), calls=%async_computation.2 | async-start | bytes 16384 | tf_op jit(solution)/shard_map/all_to_all | solution.py:100
  26.9 9.3 %all_gather.9 = bf16[256,512]{1,0:T(8,128)(2,1)S(1)} all-gather(bf16[32,512]{1,0:T(8,128)(2,1)S(1)} %copy-done.28), channel_id=1, replica_groups=mesh['head'=4,'tok'=8] {'tok'}, dimensions={0}, use_global_device_ids=true | all-gather | bytes 294912 | tf_op jit(solution)/shard_map/all_gather | solution.py:20
  36.4 0.6 copy.35
  37.0 0.3 fusion.83
  37.4 1.3 fusion.84
  38.6 1.3 fusion.85
  39.9 1.3 fusion.86
  41.2 1.3 fusion.87
  42.5 0.3 fusion.88
  42.8 0.3 fusion.89
  43.1 1.2 fusion.90
  44.6 8.5 %all_gather.10 = bf16[256,512]{1,0:T(8,128)(2,1)S(1)} all-gather(bf16[32,512]{1,0:T(8,128)(2,1)S(1)} %copy-done.29), channel_id=1, replica_groups=mesh['head'=4,'tok'=8] {'tok'}, dimensions={0}, use_global_device_ids=true | all-gather | bytes 294912 | tf_op jit(solution)/shard_map/all_gather | solution.py:21
  53.3 1.5 %fusion.28 = f32[896]{0:T(1024)S(1)} fusion(f32[896,256]{0,1:T(8,128)} %get-tuple-element.39, f32[896]{0:T(1024)S(1)} %broadcast_maximum_fusion.6), kind=kLoop, calls=%fused_computation.81 | loop fusion | flops 457856 | bytes 924672 | tf_op jit(solution)/shard_map/reduce_sum | solution.py:44
  54.7 1.3 fusion.30
  56.1 0.6 fusion.77
  56.8 0.6 fusion.78
  57.6 0.6 fusion.79
  58.4 0.6 fusion.80
  59.2 0.6 fusion.81
  59.8 0.8 fusion.42
  60.6 1.6 %fusion.44 = (f32[256]{0:T(256)}, bf16[256,896]{1,0:T(8,128)(2,1)}) fusion(f32[256,896]{1,0:T(8,128)S(1)} %copy-done.13, f32[256]{0:T(256)S(1)} %copy-done.48), kind=kLoop, calls=%fused_computation.97 | loop fusion | flops 687872 | bytes 1378304 | tf_op jit(solution)/shard_map/reduce_sum | solution.py:84
  62.2 1.6 %fusion.46 = (f32[256]{0:T(256)}, bf16[256,896]{1,0:T(8,128)(2,1)}) fusion(f32[256,896]{1,0:T(8,128)S(1)} %copy-done.12, f32[256]{0:T(256)S(1)} %copy-done.46), kind=kLoop, calls=%fused_computation.99 | loop fusion | flops 687872 | bytes 1378304 | tf_op jit(solution)/shard_map/reduce_sum | solution.py:84
  63.8 1.6 %fusion.48 = (f32[256]{0:T(256)}, bf16[256,896]{1,0:T(8,128)(2,1)}) fusion(f32[256,896]{1,0:T(8,128)S(1)} %copy-done.11, f32[256]{0:T(256)S(1)} %copy-done.44), kind=kLoop, calls=%fused_computation.101 | loop fusion | flops 687872 | bytes 1378304 | tf_op jit(solution)/shard_map/reduce_sum | solution.py:84
  65.4 1.5 %fusion.50 = (f32[256]{0:T(256)}, bf16[256,896]{1,0:T(8,128)(2,1)}) fusion(f32[256,896]{1,0:T(8,128)S(1)} %copy-done.10, f32[256]{0:T(256)S(1)} %copy-done.42), kind=kLoop, calls=%fused_computation.103 | loop fusion | flops 687872 | bytes 1378304 | tf_op jit(solution)/shard_map/reduce_sum | solution.py:84
  67.0 1.6 %fusion.52 = (f32[256]{0:T(256)}, bf16[256,896]{1,0:T(8,128)(2,1)}) fusion(f32[256,896]{1,0:T(8,128)S(1)} %copy-done.9, f32[256]{0:T(256)S(1)} %copy-done.40), kind=kLoop, calls=%fused_computation.105 | loop fusion | flops 687872 | bytes 1378304 | tf_op jit(solution)/shard_map/reduce_sum | solution.py:84
  68.6 1.6 %fusion.54 = (f32[256]{0:T(256)}, bf16[256,896]{1,0:T(8,128)(2,1)}) fusion(f32[256,896]{1,0:T(8,128)S(1)} %copy-done.8, f32[256]{0:T(256)S(1)} %copy-done.38), kind=kLoop, calls=%fused_computation.107 | loop fusion | flops 687872 | bytes 1378304 | tf_op jit(solution)/shard_map/reduce_sum | solution.py:84
  70.2 1.5 %fusion.56 = (f32[256]{0:T(256)}, bf16[256,896]{1,0:T(8,128)(2,1)}) fusion(f32[256,896]{1,0:T(8,128)S(1)} %copy-done.7, f32[256]{0:T(256)S(1)} %copy-done.36), kind=kLoop, calls=%fused_computation.109 | loop fusion | flops 687872 | bytes 1378304 | tf_op jit(solution)/shard_map/reduce_sum | solution.py:84
  71.7 2.2 %copy.42 = bf16[896,512]{0,1:T(8,128)(2,1)} copy(bf16[896,512]{1,0:T(8,128)(2,1)} %param.9) | data formatting | bytes 1835008 | tf_op args[2]
  73.9 1.6 %fusion.16 = f32[8,896,64]{1,2,0:T(8,128)S(1)} fusion(f32[896,256]{0,1:T(8,128)} %copy-done.5, f32[896]{0:T(1024)S(1)} %broadcast_maximum_fusion.7, f32[896]{0:T(1024)S(1)} %get-tuple-element.35, bf16[256,8,64]{0,2,1:T(8,128)(2,1)S(1)} %bitcast.365), kind=kOutput, calls=%fused_computation.44 | convolution fusion | flops 29876224 | bytes 1187840 | tf_op jit(solution)/shard_map/dot_general | solution.py:47
  75.5 1.5 %fusion.14 = f32[8,896,64]{1,2,0:T(8,128)S(1)} fusion(f32[8,896,64]{1,2,0:T(8,128)S(1)} %fusion.16, f32[896,256]{0,1:T(8,128)} %get-tuple-element.39, f32[896]{0:T(1024)S(1)} %broadcast_maximum_fusion.6, f32[896]{0:T(1024)S(1)} %get-tuple-element.33, bf16[256,8,64]{0,2,1:T(8,128)(2,1)S(1)} %bitcast.366), kind=kOutput, calls=%fused_computation.41 | convolution fusion | flops 29876224 | bytes 1187840 | tf_op jit(solution)/shard_map/dot_general | solution.py:47
  81.2 1.0 copy-done.24
  83.1 0.7 reshape.487
  83.7 4.7 %all-to-all-start.3 = ((f32[8,1,256]{2,1,0:T(1,128)}), f32[8,1,256]{2,1,0:T(1,128)S(1)}, u32[]{:S(2)}, u32[]{:S(2)}) async-start(f32[8,1,256]{2,1,0:T(1,128)} %reshape.487), calls=%async_computation.3 | async-start | bytes 16384 | tf_op jit(solution)/shard_map/all_to_all | solution.py:101
  88.7 1.5 %reshape.483 = f32[8,1,16384]{2,1,0:T(1,128)} reshape(f32[8,8,32,64]{3,2,1,0:T(8,128)S(1)} %bitcast.332) | data formatting | bytes 1048576
  90.2 1.5 %all-to-all-done.3 = f32[8,1,256]{2,1,0:T(1,128)S(1)} async-done(((f32[8,1,256]{2,1,0:T(1,128)}), f32[8,1,256]{2,1,0:T(1,128)S(1)}, u32[]{:S(2)}, u32[]{:S(2)}) %all-to-all-start.3) | async-done | bytes 8224 | tf_op jit(solution)/shard_map/all_to_all | solution.py:101
  91.7 4.9 %all-to-all-start.1 = ((f32[8,1,16384]{2,1,0:T(1,128)}), f32[8,1,16384]{2,1,0:T(1,128)S(1)}, u32[]{:S(2)}, u32[]{:S(2)}) async-start(f32[8,1,16384]{2,1,0:T(1,128)} %reshape.483), calls=%async_computation.1 | async-start | bytes 1048576 | tf_op jit(solution)/shard_map/all_to_all | solution.py:102
  96.6 1.0 fusion.2
  97.6 1.7 %fusion.25 = bf16[896,8,64]{0,2,1:T(8,128)(2,1)S(1)} fusion(f32[8,896,64]{1,2,0:T(8,128)} %fusion.2, f32[8,896]{1,0:T(8,128)S(1)} %stack.112), kind=kLoop, calls=%fused_computation.78 | loop fusion | flops 917504 | bytes 2781184 | tf_op jit(solution)/shard_map/convert_element_type | solution.py:59
  99.2 0.9 convert_element_type.94
  100.1 1.4 %copy.38 = bf16[4,224,512]{2,1,0:T(8,128)(2,1)} copy(bf16[4,224,512]{1,0,2:T(4,128)(2,1)S(1)} %convert_element_type.94) | data formatting | bytes 1835008 | tf_op jit(solution)/shard_map/convert_element_type | solution.py:59
  101.5 3.4 %all-to-all-done.1 = f32[8,1,16384]{2,1,0:T(1,128)S(1)} async-done(((f32[8,1,16384]{2,1,0:T(1,128)}), f32[8,1,16384]{2,1,0:T(1,128)S(1)}, u32[]{:S(2)}, u32[]{:S(2)}) %all-to-all-start.1) | async-done | bytes 524320 | tf_op jit(solution)/shard_map/all_to_all | solution.py:102
  104.9 4.9 %all-to-all-start = ((bf16[4,224,512]{2,1,0:T(8,128)(2,1)}), bf16[4,224,512]{2,1,0:T(8,128)(2,1)S(1)}, u32[]{:S(2)}, u32[]{:S(2)}) async-start(bf16[4,224,512]{2,1,0:T(8,128)(2,1)} %copy.38), calls=%async_computation | async-start | bytes 1835008 | tf_op jit(solution)/shard_map/all_to_all | solution.py:62
  109.7 0.5 broadcast.428
  110.2 0.7 reduce.3
  111.0 0.7 reduce.4
  111.8 1.9 %reduce.5 = f32[8,16384]{1,0:T(8,128)S(1)} reduce(f32[8,1,16384]{2,1,0:T(1,128)S(1)} %all-to-all-done.1, f32[]{:T(128)} %broadcast.428), dimensions={1}, to_apply=%all_to_all.17.reduce_sub_computation | reduce | bytes 1048580 | tf_op jit(solution)/shard_map/all_to_all | solution.py:102
  113.7 0.4 reshape.484
  114.1 0.3 multiply_reduce_fusion
  114.6 0.7 convert_element_type.110
  115.3 17.6 %all-to-all-done = bf16[4,224,512]{2,1,0:T(8,128)(2,1)S(1)} async-done(((bf16[4,224,512]{2,1,0:T(8,128)(2,1)}), bf16[4,224,512]{2,1,0:T(8,128)(2,1)S(1)}, u32[]{:S(2)}, u32[]{:S(2)}) %all-to-all-start) | async-done | bytes 917536 | tf_op jit(solution)/shard_map/all_to_all | solution.py:62
  133.1 1.2 copy.39
  134.3 0.7 copy.49
  135.4 1.1 multiply_convert_fusion
  (190 shorter events, 7.8 us)
Async XLA Ops:
  0.6 1.6 %copy-start.27 = (bf16[32,512]{1,0:T(8,128)(2,1)S(1)}, bf16[32,512]{1,0:T(8,128)(2,1)}, u32[]{:S(2)}) copy-start(bf16[32,512]{1,0:T(8,128)(2,1)} %param.10) | copy-start | bytes 98308
  12.9 8.8 %copy-start.49 = (f32[256]{0:T(256)}, f32[256]{0:T(256)S(1)}, u32[]{:S(2)}) copy-start(f32[256]{0:T(256)S(1)} %get-tuple-element.52) | copy-start | bytes 3076
  14.2 7.7 %copy-start.47 = (f32[256]{0:T(256)}, f32[256]{0:T(256)S(1)}, u32[]{:S(2)}) copy-start(f32[256]{0:T(256)S(1)} %get-tuple-element.54) | copy-start | bytes 3076
  15.5 6.4 %copy-start.45 = (f32[256]{0:T(256)}, f32[256]{0:T(256)S(1)}, u32[]{:S(2)}) copy-start(f32[256]{0:T(256)S(1)} %get-tuple-element.56) | copy-start | bytes 3076
  16.7 5.3 %copy-start.43 = (f32[256]{0:T(256)}, f32[256]{0:T(256)S(1)}, u32[]{:S(2)}) copy-start(f32[256]{0:T(256)S(1)} %get-tuple-element.58) | copy-start | bytes 3076
  18.0 18.2 %copy-start.41 = (f32[256]{0:T(256)}, f32[256]{0:T(256)S(1)}, u32[]{:S(2)}) copy-start(f32[256]{0:T(256)S(1)} %get-tuple-element.60) | copy-start | bytes 3076
  18.0 9.0 %copy-start.28 = (bf16[32,512]{1,0:T(8,128)(2,1)S(1)}, bf16[32,512]{1,0:T(8,128)(2,1)}, u32[]{:S(2)}) copy-start(bf16[32,512]{1,0:T(8,128)(2,1)} %param.11) | copy-start | bytes 98308
  18.0 18.4 %copy-start.26 = (bf16[896,512]{1,0:T(8,128)(2,1)S(1)}, bf16[896,512]{1,0:T(8,128)(2,1)}, u32[]{:S(2)}) copy-start(bf16[896,512]{1,0:T(8,128)(2,1)} %param.7) | copy-start | bytes 2752516
  19.2 17.7 %copy-start.39 = (f32[256]{0:T(256)}, f32[256]{0:T(256)S(1)}, u32[]{:S(2)}) copy-start(f32[256]{0:T(256)S(1)} %get-tuple-element.62) | copy-start | bytes 3076
  20.5 16.5 %copy-start.37 = (f32[256]{0:T(256)}, f32[256]{0:T(256)S(1)}, u32[]{:S(2)}) copy-start(f32[256]{0:T(256)S(1)} %get-tuple-element.64) | copy-start | bytes 3076
  21.7 15.6 %copy-start.35 = (f32[256]{0:T(256)}, f32[256]{0:T(256)S(1)}, u32[]{:S(2)}) copy-start(f32[256]{0:T(256)S(1)} %get-tuple-element.66) | copy-start | bytes 3076
  23.2 60.6 %all-to-all-start.2 = ((f32[8,1,256]{2,1,0:T(1,128)}), f32[8,1,256]{2,1,0:T(1,128)S(1)}, u32[]{:S(2)}, u32[]{:S(2)}) async-start(f32[8,1,256]{2,1,0:T(1,128)} %reshape.485), calls=%async_computation.2 | async-start | bytes 16384 | tf_op jit(solution)/shard_map/all_to_all | solution.py:100
  37.0 5.8 %copy-start.6 = (bf16[896,512]{0,1:T(8,128)(2,1)}, bf16[896,512]{0,1:T(8,128)(2,1)S(1)}, u32[]{:S(2)}) copy-start(bf16[896,512]{0,1:T(8,128)(2,1)S(1)} %copy.35) | copy-start | bytes 2752516
  37.3 7.0 %copy-start.5 = (f32[896,256]{0,1:T(8,128)}, f32[896,256]{0,1:T(8,128)S(1)}, u32[]{:S(2)}) copy-start(f32[896,256]{0,1:T(8,128)S(1)} %get-tuple-element.37) | copy-start | bytes 2752516
  42.4 2.1 %copy-start.29 = (bf16[32,512]{1,0:T(8,128)(2,1)S(1)}, bf16[32,512]{1,0:T(8,128)(2,1)}, u32[]{:S(2)}) copy-start(bf16[32,512]{1,0:T(8,128)(2,1)} %param.12) | copy-start | bytes 98308
  53.2 3.4 %copy-start.2 = (f32[896,256]{0,1:T(8,128)S(1)}, f32[896,256]{0,1:T(8,128)}, u32[]{:S(2)}) copy-start(f32[896,256]{0,1:T(8,128)} %get-tuple-element.43) | copy-start | bytes 2752516
  53.2 4.2 %copy-start = (f32[896,256]{0,1:T(8,128)S(1)}, f32[896,256]{0,1:T(8,128)}, u32[]{:S(2)}) copy-start(f32[896,256]{0,1:T(8,128)} %get-tuple-element.45) | copy-start | bytes 2752516
  56.7 3.1 %copy-start.14 = (f32[256,896]{1,0:T(8,128)S(1)}, f32[256,896]{1,0:T(8,128)}, u32[]{:S(2)}) copy-start(f32[256,896]{1,0:T(8,128)} %get-tuple-element.53) | copy-start | bytes 2752516
  56.7 3.1 %copy-start.50 = (f32[256]{0:T(256)S(1)}, f32[256]{0:T(256)}, u32[]{:S(2)}) copy-start(f32[256]{0:T(256)} %copy-done.49) | copy-start | bytes 3076
  57.6 3.0 %copy-start.13 = (f32[256,896]{1,0:T(8,128)S(1)}, f32[256,896]{1,0:T(8,128)}, u32[]{:S(2)}) copy-start(f32[256,896]{1,0:T(8,128)} %get-tuple-element.55) | copy-start | bytes 2752516
  57.6 3.0 %copy-start.48 = (f32[256]{0:T(256)S(1)}, f32[256]{0:T(256)}, u32[]{:S(2)}) copy-start(f32[256]{0:T(256)} %copy-done.47) | copy-start | bytes 3076
  59.0 3.2 %copy-start.12 = (f32[256,896]{1,0:T(8,128)S(1)}, f32[256,896]{1,0:T(8,128)}, u32[]{:S(2)}) copy-start(f32[256,896]{1,0:T(8,128)} %get-tuple-element.57) | copy-start | bytes 2752516
  59.0 3.2 %copy-start.46 = (f32[256]{0:T(256)S(1)}, f32[256]{0:T(256)}, u32[]{:S(2)}) copy-start(f32[256]{0:T(256)} %copy-done.45) | copy-start | bytes 3076
  59.8 4.1 %copy-start.11 = (f32[256,896]{1,0:T(8,128)S(1)}, f32[256,896]{1,0:T(8,128)}, u32[]{:S(2)}) copy-start(f32[256,896]{1,0:T(8,128)} %get-tuple-element.59) | copy-start | bytes 2752516
  59.8 4.1 %copy-start.44 = (f32[256]{0:T(256)S(1)}, f32[256]{0:T(256)}, u32[]{:S(2)}) copy-start(f32[256]{0:T(256)} %copy-done.43) | copy-start | bytes 3076
  60.6 4.8 %copy-start.10 = (f32[256,896]{1,0:T(8,128)S(1)}, f32[256,896]{1,0:T(8,128)}, u32[]{:S(2)}) copy-start(f32[256,896]{1,0:T(8,128)} %get-tuple-element.61) | copy-start | bytes 2752516
  60.6 4.8 %copy-start.42 = (f32[256]{0:T(256)S(1)}, f32[256]{0:T(256)}, u32[]{:S(2)}) copy-start(f32[256]{0:T(256)} %copy-done.41) | copy-start | bytes 3076
  62.2 4.8 %copy-start.9 = (f32[256,896]{1,0:T(8,128)S(1)}, f32[256,896]{1,0:T(8,128)}, u32[]{:S(2)}) copy-start(f32[256,896]{1,0:T(8,128)} %get-tuple-element.63) | copy-start | bytes 2752516
  62.2 4.8 %copy-start.40 = (f32[256]{0:T(256)S(1)}, f32[256]{0:T(256)}, u32[]{:S(2)}) copy-start(f32[256]{0:T(256)} %copy-done.39) | copy-start | bytes 3076
  63.8 4.8 %copy-start.8 = (f32[256,896]{1,0:T(8,128)S(1)}, f32[256,896]{1,0:T(8,128)}, u32[]{:S(2)}) copy-start(f32[256,896]{1,0:T(8,128)} %get-tuple-element.65) | copy-start | bytes 2752516
  63.8 4.8 %copy-start.38 = (f32[256]{0:T(256)S(1)}, f32[256]{0:T(256)}, u32[]{:S(2)}) copy-start(f32[256]{0:T(256)} %copy-done.37) | copy-start | bytes 3076
  65.4 4.7 %copy-start.7 = (f32[256,896]{1,0:T(8,128)S(1)}, f32[256,896]{1,0:T(8,128)}, u32[]{:S(2)}) copy-start(f32[256,896]{1,0:T(8,128)} %get-tuple-element.67) | copy-start | bytes 2752516
  65.4 4.7 %copy-start.36 = (f32[256]{0:T(256)S(1)}, f32[256]{0:T(256)}, u32[]{:S(2)}) copy-start(f32[256]{0:T(256)} %copy-done.35) | copy-start | bytes 3076
  73.9 3.1 %copy-start.4 = (f32[896,256]{0,1:T(8,128)S(1)}, f32[896,256]{0,1:T(8,128)}, u32[]{:S(2)}) copy-start(f32[896,256]{0,1:T(8,128)} %get-tuple-element.41) | copy-start | bytes 2752516
  73.9 3.4 %copy-start.3 = (f32[896,256]{0,1:T(8,128)S(1)}, f32[896,256]{0,1:T(8,128)}, u32[]{:S(2)}) copy-start(f32[896,256]{0,1:T(8,128)} %get-tuple-element.43) | copy-start | bytes 2752516
  75.5 2.1 %copy-start.1 = (f32[896,256]{0,1:T(8,128)S(1)}, f32[896,256]{0,1:T(8,128)}, u32[]{:S(2)}) copy-start(f32[896,256]{0,1:T(8,128)} %get-tuple-element.45) | copy-start | bytes 2752516
  77.6 1.2 copy-start.15
  77.9 1.2 copy-start.17
  77.9 1.5 %copy-start.18 = (bf16[256,896]{1,0:T(8,128)(2,1)S(1)}, bf16[256,896]{1,0:T(8,128)(2,1)}, u32[]{:S(2)}) copy-start(bf16[256,896]{1,0:T(8,128)(2,1)} %get-tuple-element.15) | copy-start | bytes 1376260
  78.1 1.5 %copy-start.19 = (bf16[256,896]{1,0:T(8,128)(2,1)S(1)}, bf16[256,896]{1,0:T(8,128)(2,1)}, u32[]{:S(2)}) copy-start(bf16[256,896]{1,0:T(8,128)(2,1)} %get-tuple-element.13) | copy-start | bytes 1376260
  78.2 1.7 %copy-start.20 = (bf16[256,896]{1,0:T(8,128)(2,1)S(1)}, bf16[256,896]{1,0:T(8,128)(2,1)}, u32[]{:S(2)}) copy-start(bf16[256,896]{1,0:T(8,128)(2,1)} %get-tuple-element.11) | copy-start | bytes 1376260
  78.4 2.1 %copy-start.16 = (f32[8,896,64]{1,2,0:T(8,128)}, f32[8,896,64]{1,2,0:T(8,128)S(1)}, u32[]{:S(2)}) copy-start(f32[8,896,64]{1,2,0:T(8,128)S(1)} %fusion.4) | copy-start | bytes 5505028
  78.4 1.9 %copy-start.21 = (bf16[256,896]{1,0:T(8,128)(2,1)S(1)}, bf16[256,896]{1,0:T(8,128)(2,1)}, u32[]{:S(2)}) copy-start(bf16[256,896]{1,0:T(8,128)(2,1)} %get-tuple-element.9) | copy-start | bytes 1376260
  79.0 1.6 %copy-start.22 = (bf16[256,896]{1,0:T(8,128)(2,1)S(1)}, bf16[256,896]{1,0:T(8,128)(2,1)}, u32[]{:S(2)}) copy-start(bf16[256,896]{1,0:T(8,128)(2,1)} %get-tuple-element.7) | copy-start | bytes 1376260
  79.3 1.6 %copy-start.23 = (bf16[256,896]{1,0:T(8,128)(2,1)S(1)}, bf16[256,896]{1,0:T(8,128)(2,1)}, u32[]{:S(2)}) copy-start(bf16[256,896]{1,0:T(8,128)(2,1)} %get-tuple-element.5) | copy-start | bytes 1376260
  79.9 2.4 %copy-start.52 = (f32[256]{0:T(256)S(1)}, f32[256]{0:T(256)}, u32[]{:S(2)}) copy-start(f32[256]{0:T(256)} %get-tuple-element.18) | copy-start | bytes 3076
  79.9 2.5 %copy-start.53 = (f32[256]{0:T(256)S(1)}, f32[256]{0:T(256)}, u32[]{:S(2)}) copy-start(f32[256]{0:T(256)} %get-tuple-element.16) | copy-start | bytes 3076
  79.9 2.6 %copy-start.54 = (f32[256]{0:T(256)S(1)}, f32[256]{0:T(256)}, u32[]{:S(2)}) copy-start(f32[256]{0:T(256)} %get-tuple-element.14) | copy-start | bytes 3076
  79.9 2.6 %copy-start.55 = (f32[256]{0:T(256)S(1)}, f32[256]{0:T(256)}, u32[]{:S(2)}) copy-start(f32[256]{0:T(256)} %get-tuple-element.12) | copy-start | bytes 3076
  79.9 2.7 %copy-start.56 = (f32[256]{0:T(256)S(1)}, f32[256]{0:T(256)}, u32[]{:S(2)}) copy-start(f32[256]{0:T(256)} %get-tuple-element.10) | copy-start | bytes 3076
  79.9 2.8 %copy-start.57 = (f32[256]{0:T(256)S(1)}, f32[256]{0:T(256)}, u32[]{:S(2)}) copy-start(f32[256]{0:T(256)} %get-tuple-element.8) | copy-start | bytes 3076
  80.0 2.9 %copy-start.58 = (f32[256]{0:T(256)S(1)}, f32[256]{0:T(256)}, u32[]{:S(2)}) copy-start(f32[256]{0:T(256)} %get-tuple-element.6) | copy-start | bytes 3076
  80.0 2.9 %copy-start.59 = (f32[256]{0:T(256)S(1)}, f32[256]{0:T(256)}, u32[]{:S(2)}) copy-start(f32[256]{0:T(256)} %get-tuple-element.4) | copy-start | bytes 3076
  80.0 8.5 %copy-start.30 = (f32[896]{0:T(1024)S(1)}, f32[896]{0:T(1024)}, u32[]{:S(2)}) copy-start(f32[896]{0:T(1024)} %get-tuple-element.30) | copy-start | bytes 10756
  80.0 8.5 %copy-start.31 = (f32[896]{0:T(1024)S(1)}, f32[896]{0:T(1024)}, u32[]{:S(2)}) copy-start(f32[896]{0:T(1024)} %get-tuple-element.28) | copy-start | bytes 10756
  80.0 8.5 %copy-start.32 = (f32[896]{0:T(1024)S(1)}, f32[896]{0:T(1024)}, u32[]{:S(2)}) copy-start(f32[896]{0:T(1024)} %get-tuple-element.26) | copy-start | bytes 10756
  80.0 8.6 %copy-start.33 = (f32[896]{0:T(1024)S(1)}, f32[896]{0:T(1024)}, u32[]{:S(2)}) copy-start(f32[896]{0:T(1024)} %get-tuple-element.24) | copy-start | bytes 10756
  80.0 8.6 %copy-start.34 = (f32[896]{0:T(1024)S(1)}, f32[896]{0:T(1024)}, u32[]{:S(2)}) copy-start(f32[896]{0:T(1024)} %get-tuple-element.22) | copy-start | bytes 10756
  81.1 1.0 copy-start.24
  82.1 6.5 %copy-start.25 = (f32[8,8,32,64]{3,2,1,0:T(8,128)S(1)}, f32[8,8,32,64]{3,2,1,0:T(8,128)}, u32[]{:S(2)}) copy-start(f32[8,8,32,64]{3,2,1,0:T(8,128)} %copy-done.24) | copy-start | bytes 1572868
  83.7 8.0 %all-to-all-start.3 = ((f32[8,1,256]{2,1,0:T(1,128)}), f32[8,1,256]{2,1,0:T(1,128)S(1)}, u32[]{:S(2)}, u32[]{:S(2)}) async-start(f32[8,1,256]{2,1,0:T(1,128)} %reshape.487), calls=%async_computation.3 | async-start | bytes 16384 | tf_op jit(solution)/shard_map/all_to_all | solution.py:101
  91.7 13.1 %all-to-all-start.1 = ((f32[8,1,16384]{2,1,0:T(1,128)}), f32[8,1,16384]{2,1,0:T(1,128)S(1)}, u32[]{:S(2)}, u32[]{:S(2)}) async-start(f32[8,1,16384]{2,1,0:T(1,128)} %reshape.483), calls=%async_computation.1 | async-start | bytes 1048576 | tf_op jit(solution)/shard_map/all_to_all | solution.py:102
  104.9 28.0 %all-to-all-start = ((bf16[4,224,512]{2,1,0:T(8,128)(2,1)}), bf16[4,224,512]{2,1,0:T(8,128)(2,1)S(1)}, u32[]{:S(2)}, u32[]{:S(2)}) async-start(bf16[4,224,512]{2,1,0:T(8,128)(2,1)} %copy.38), calls=%async_computation | async-start | bytes 1835008 | tf_op jit(solution)/shard_map/all_to_all | solution.py:62
  134.3 1.0 copy-start.51
where the time goes:
time: 137 us
  blocking collectives  27.1 us (20%)
  other arithmetic  25.6 us (19%)
  matrix products  24.9 us (18%)
  waiting for transfers between devices  22.4 us (16%)
  starting transfers between devices  18.2 us (13%)
  local copies, waits for them, and re-layouts  16.8 us (12%)
  between operations  1.52 us (1%)
    all_to_all x1, waiting for transfers between devices, shards(): lax.all_to_all(pieces, 'head', split_axis=0, concat_axis=2, tiled=True)  17.6 us
    reduce_sum x8, other arithmetic, shards(): sum_list.append(jnp.sum(weights, axis=1))  11.8 us
    dot_general x8, matrix products, shards(): jnp.einsum('qd,kd->qk', all_queries[:, head_index], video_keys[:, head_in...  10.1 us
    unnamed x130, local copies, waits for them, and re-layouts  10 us
    all_gather x1, blocking collectives, shards(): lax.all_gather(audio_q, 'tok', axis=0, tiled=True)  9.31 us
    all_gather x1, blocking collectives, shards(): lax.all_gather(audio_k, 'tok', axis=0, tiled=True)  9.26 us
    all_gather x1, blocking collectives, shards(): lax.all_gather(audio_v, 'tok', axis=0, tiled=True)  8.52 us
    dot_general x8, matrix products, shards(): jnp.einsum('qd,kd->qk', video_heads[:, absorb_head_index], key_block[:, a...  7.34 us
  transfers between devices with their start and end apart: 4, of which 3 were waited for; matrix products, arithmetic and copies ran while one was open for 36% of the time, Pallas kernels for 0%

commit v1 on v0

--- a/solution.py
+++ b/solution.py
@@ -4,6 +4,11 @@
 from jax.sharding import PartitionSpec as P
 
 HEAD_DIM = 64
+
+
+def exchange_gather(block, name, dim):
+    sent = jnp.stack([block] * lax.axis_size(name))
+    return jnp.concatenate(lax.all_to_all(sent, name, 0, 0), axis=dim)
 
 
 def shards(video_q, video_k, video_v, audio_q, audio_k, audio_v, norm_gain):
@@ -64,7 +69,7 @@
     widened = normalize_received.astype(jnp.float32)
     mean_square = jnp.mean(widened * widened, axis=-1, keepdims=True)
     video_out = (widened * lax.rsqrt(mean_square + 1e-06) * norm_gain).astype(jnp.bfloat16)
-    all_queries = split_heads(lax.all_gather(audio_q, "tok", axis=0, tiled=True))
+    all_queries = split_heads(exchange_gather(audio_q, "tok", 0))
     video_keys = split_heads(video_k)
     video_values = split_heads(video_v)
     max_list, sum_list, out_list = ([], [], [])

time: 137 us -> 151 us (1.10)
  matrix products: 24.9 us -> 39.9 us
  local copies, waits for them, and re-layouts: 16.8 us -> 31.6 us
  other arithmetic: 25.6 us -> 15.8 us
  blocking collectives: 27.1 us -> 18.3 us
  starting transfers between devices: 18.2 us -> 21.7 us
    reduce_sum x8, other arithmetic: 11.8 us -> 2.38 us  [shards(): sum_list.append(jnp.sum(weights, axis=1))]
    all_gather x1 -> x0, blocking collectives: 9.31 us -> none  [shards(): lax.all_gather(audio_q, 'tok', axis=0, tiled=True)]
    dot_general x8, matrix products: 10.1 us -> 17.2 us  [shards(): jnp.einsum('qd,kd->qk', all_queries[:, head_index], video_keys[:, head_in...]
    slice x0 -> x9, local copies, waits for them, and re-layouts: none -> 6.69 us  [shards(): all_queries[:, head_index]]
    dot_general x8, matrix products: 5.39 us -> 10.2 us  [shards(): jnp.dot(absorb_weights.astype(jnp.bfloat16), value_block[:, absorb_head_i...]
    all_to_all x0 -> x1, starting transfers between devices: none -> 4.25 us  [exchange_gather(): return jnp.concatenate(lax.all_to_all(sent, name, 0, 0), axis=dim)]
    another operation x9, local copies, waits for them, and re-layouts: 0.73 us -> 3.82 us  [shards(): part_max = jnp.stack(max_list)]
    dot_general x8, matrix products: 7.34 us -> 9.68 us  [shards(): jnp.einsum('qd,kd->qk', video_heads[:, absorb_head_index], key_block[:, a...]
  transfers between devices with their start and end apart: 4 -> 5, of which waited for: 3 -> 2; matrix products, arithmetic and copies ran while one was open for 36% -> 34% of each run, Pallas kernels for 0% -> 0%
where the time goes in v1:
time: 151 us; the launch traced here: 150 us
  matrix products  39.9 us (26%)
  local copies, waits for them, and re-layouts  31.6 us (21%)
  starting transfers between devices  21.7 us (14%)
  waiting for transfers between devices  20.9 us (14%)
  blocking collectives  18.3 us (12%)
  other arithmetic  15.8 us (10%)
    all_to_all x1, waiting for transfers between devices, shards(): lax.all_to_all(pieces, 'head', split_axis=0, concat_axis=2, tiled=True)  17.6 us
    dot_general x8, matrix products, shards(): jnp.einsum('qd,kd->qk', all_queries[:, head_index], video_keys[:, head_in...  17.2 us
    unnamed x72, local copies, waits for them, and re-layouts  11.6 us
    dot_general x8, matrix products, shards(): jnp.dot(absorb_weights.astype(jnp.bfloat16), value_block[:, absorb_head_i...  10.2 us
    dot_general x8, matrix products, shards(): jnp.einsum('qd,kd->qk', video_heads[:, absorb_head_index], key_block[:, a...  9.68 us
    all_gather x1, blocking collectives, shards(): lax.all_gather(audio_k, 'tok', axis=0, tiled=True)  9.24 us
    all_gather x1, blocking collectives, shards(): lax.all_gather(audio_v, 'tok', axis=0, tiled=True)  9.09 us
    slice x9, local copies, waits for them, and re-layouts, shards(): all_queries[:, head_index]  6.69 us
  transfers between devices with their start and end apart: 5, of which 2 were waited for; matrix products, arithmetic and copies ran while one was open for 34% of the time, Pallas kernels for 0%

profile of v1, /device:TPU:2, one launch (start us, length us, event | category | flops | bytes accessed | tf_op | source)
XLA Modules:
  0.0 149.6 jit_solution(4969228575760090375)
XLA Ops:
  0.6 1.6 %stack.124 = bf16[8,32,512]{2,1,0:T(8,128)(2,1)} broadcast(bf16[32,512]{1,0:T(8,128)(2,1)} %param.10), dimensions={1,2} | broadcast | bytes 294912 | tf_op jit(solution)/shard_map/stack | solution.py:10
  2.2 4.3 %all-to-all-start.1 = ((bf16[8,32,512]{2,1,0:T(8,128)(2,1)}), bf16[8,32,512]{2,1,0:T(8,128)(2,1)S(1)}, u32[]{:S(2)}, u32[]{:S(2)}) async-start(bf16[8,32,512]{2,1,0:T(8,128)(2,1)} %stack.124), calls=%async_computation.1 | async-start | bytes 524288 | tf_op jit(solution)/shard_map/all_to_all | solution.py:11
  6.5 9.2 %all_gather.6 = bf16[256,512]{1,0:T(8,128)(2,1)S(1)} all-gather(bf16[32,512]{1,0:T(8,128)(2,1)} %param.11), channel_id=1, replica_groups=mesh['head'=4,'tok'=8] {'tok'}, dimensions={0}, use_global_device_ids=true | all-gather | bytes 294912 | tf_op jit(solution)/shard_map/all_gather | solution.py:25
  16.8 1.9 %fusion.93 = (f32[896]{0:T(1024)}, f32[896,256]{0,1:T(8,128)}) fusion(bf16[256,8,64]{0,2,1:T(8,128)(2,1)S(1)} %bitcast.373, bf16[896,8,64]{0,2,1:T(8,128)(2,1)S(1)} %bitcast.341), kind=kOutput, calls=%fused_computation.198 | convolution fusion | flops 29817984 | bytes 1068544 | tf_op jit(solution)/shard_map/qd,kd->qk/dot_general | solution.py:38
  18.7 1.9 %fusion.94 = (f32[896]{0:T(1024)}, f32[896,256]{0,1:T(8,128)}) fusion(bf16[256,8,64]{0,2,1:T(8,128)(2,1)S(1)} %bitcast.374, bf16[896,8,64]{0,2,1:T(8,128)(2,1)S(1)} %bitcast.342), kind=kOutput, calls=%fused_computation.199 | convolution fusion | flops 29817984 | bytes 1068544 | tf_op jit(solution)/shard_map/qd,kd->qk/dot_general | solution.py:38
  20.6 1.9 %fusion.95 = (f32[896]{0:T(1024)}, f32[896,256]{0,1:T(8,128)}) fusion(bf16[256,8,64]{0,2,1:T(8,128)(2,1)S(1)} %bitcast.375, bf16[896,8,64]{0,2,1:T(8,128)(2,1)S(1)} %bitcast.343), kind=kOutput, calls=%fused_computation.200 | convolution fusion | flops 29817984 | bytes 1068544 | tf_op jit(solution)/shard_map/qd,kd->qk/dot_general | solution.py:38
  22.4 1.8 %fusion.96 = (f32[896]{0:T(1024)}, f32[896,256]{0,1:T(8,128)}) fusion(bf16[256,8,64]{0,2,1:T(8,128)(2,1)S(1)} %bitcast.376, bf16[896,8,64]{0,2,1:T(8,128)(2,1)S(1)} %bitcast.344), kind=kOutput, calls=%fused_computation.201 | convolution fusion | flops 29817984 | bytes 1068544 | tf_op jit(solution)/shard_map/qd,kd->qk/dot_general | solution.py:38
  24.9 1.2 fusion.99
  26.4 0.6 fusion.83
  27.0 9.1 %all_gather.7 = bf16[256,512]{1,0:T(8,128)(2,1)S(1)} all-gather(bf16[32,512]{1,0:T(8,128)(2,1)S(1)} %copy-done.20), channel_id=1, replica_groups=mesh['head'=4,'tok'=8] {'tok'}, dimensions={0}, use_global_device_ids=true | all-gather | bytes 294912 | tf_op jit(solution)/shard_map/all_gather | solution.py:26
  36.2 0.8 broadcast_maximum_fusion.6
  37.0 1.3 fusion.28
  38.4 0.7 fusion.84
  39.1 0.7 broadcast_maximum_fusion.5
  39.7 1.3 fusion.30
  42.1 2.2 %copy.62 = bf16[896,512]{0,1:T(8,128)(2,1)} copy(bf16[896,512]{1,0:T(8,128)(2,1)} %param.8) | data formatting | bytes 1835008 | tf_op args[1]
  44.4 2.2 %copy.63 = bf16[896,512]{0,1:T(8,128)(2,1)} copy(bf16[896,512]{1,0:T(8,128)(2,1)} %param.9) | data formatting | bytes 1835008 | tf_op args[2]
  46.6 2.3 %fusion.16 = f32[8,896,64]{1,2,0:T(8,128)} fusion(f32[896,256]{0,1:T(8,128)} %copy-done.5, f32[896]{0:T(1024)S(1)} %broadcast_maximum_fusion.7, f32[896]{0:T(1024)S(1)} %copy-done.21, bf16[256,8,64]{0,2,1:T(8,128)(2,1)S(1)} %bitcast.364), kind=kOutput, calls=%fused_computation.44 | convolution fusion | flops 29876224 | bytes 1187840 | tf_op jit(solution)/shard_map/dot_general | solution.py:52
  48.8 2.2 %fusion.14 = f32[8,896,64]{1,2,0:T(8,128)} fusion(f32[8,896,64]{1,2,0:T(8,128)} %fusion.16, f32[896,256]{0,1:T(8,128)} %get-tuple-element.47, f32[896]{0:T(1024)S(1)} %broadcast_maximum_fusion.6, f32[896]{0:T(1024)S(1)} %get-tuple-element.41, bf16[256,8,64]{0,2,1:T(8,128)(2,1)S(1)} %bitcast.365), kind=kOutput, calls=%fused_computation.41 | convolution fusion | flops 29876224 | bytes 1187840 | tf_op jit(solution)/shard_map/dot_general | solution.py:52
  51.1 1.0 fusion.12
  52.0 1.0 fusion.10
  53.0 1.0 fusion.8
  54.0 0.9 fusion.6
  54.9 0.6 stack.123
  55.5 1.0 fusion.4
  56.8 1.6 %fusion.91 = (bf16[256,1,64]{2,1,0:T(2,128)(2,1)S(1)}, bf16[256,1,64]{2,1,0:T(2,128)(2,1)S(1)}, bf16[256,1,64]{2,1,0:T(2,128)(2,1)S(1)}, bf16[256,1,64]{2,1,0:T(...) fusion(bf16[256,8,64]{2,1,0:T(8,128)(2,1)S(1)} %reshape_reshape.3), kind=kLoop, calls=%fused_computation.196 | loop fusion | bytes 524288 | tf_op jit(solution)/shard_map/slice | solution.py:80
  58.6 1.3 fusion.100
  60.0 0.7 copy.64
  60.7 1.8 %fusion.101 = (f32[256]{0:T(256)}, f32[256,896]{1,0:T(8,128)S(1)}) fusion(bf16[896,8,64]{0,2,1:T(8,128)(2,1)} %bitcast.333, bf16[256,1,64]{0,2,1:T(8,128)(2,1)} %copy.64), kind=kOutput, calls=%fused_computation.206 | convolution fusion | flops 29818624 | bytes 1065984 | tf_op jit(solution)/shard_map/qd,kd->qk/dot_general | solution.py:78
  62.5 0.7 stack.127
  63.2 1.6 %copy.65 = bf16[256,1,64]{0,2,1:T(8,128)(2,1)} copy(bf16[256,1,64]{2,1,0:T(2,128)(2,1)} %get-tuple-element.25) | data formatting | bytes 65536 | tf_op jit(solution)/shard_map/slice | solution.py:80
  64.8 2.7 %fusion.102 = (f32[256]{0:T(256)}, f32[256,896]{1,0:T(8,128)}) fusion(bf16[896,8,64]{0,2,1:T(8,128)(2,1)} %bitcast.334, bf16[256,1,64]{0,2,1:T(8,128)(2,1)} %copy.65), kind=kOutput, calls=%fused_computation.207 | convolution fusion | flops 29818624 | bytes 1065984 | tf_op jit(solution)/shard_map/qd,kd->qk/dot_general | solution.py:78
  67.5 1.3 stack.128
  68.8 1.6 %copy.66 = bf16[256,1,64]{0,2,1:T(8,128)(2,1)} copy(bf16[256,1,64]{2,1,0:T(2,128)(2,1)} %get-tuple-element.24) | data formatting | bytes 65536 | tf_op jit(solution)/shard_map/slice | solution.py:80
  70.4 2.7 %fusion.103 = (f32[256]{0:T(256)}, f32[256,896]{1,0:T(8,128)}) fusion(bf16[896,8,64]{0,2,1:T(8,128)(2,1)} %bitcast.335, bf16[256,1,64]{0,2,1:T(8,128)(2,1)} %copy.66), kind=kOutput, calls=%fused_computation.208 | convolution fusion | flops 29818624 | bytes 1065984 | tf_op jit(solution)/shard_map/qd,kd->qk/dot_general | solution.py:78
  73.2 1.3 stack.129
  74.5 0.7 copy.67
  75.2 2.2 %fusion.104 = (f32[256]{0:T(256)S(1)}, f32[256,896]{1,0:T(8,128)}) fusion(bf16[896,8,64]{0,2,1:T(8,128)(2,1)} %bitcast.336, bf16[256,1,64]{0,2,1:T(8,128)(2,1)} %copy.67), kind=kOutput, calls=%fused_computation.209 | convolution fusion | flops 29818624 | bytes 1065984 | tf_op jit(solution)/shard_map/qd,kd->qk/dot_general | solution.py:78
  77.6 2.2 %fusion.105 = (f32[256]{0:T(256)S(1)}, f32[256,896]{1,0:T(8,128)}) fusion(bf16[896,8,64]{0,2,1:T(8,128)(2,1)} %bitcast.337, bf16[256,1,64]{0,2,1:T(8,128)(2,1)S(1)} %copy.68), kind=kOutput, calls=%fused_computation.210 | convolution fusion | flops 29818624 | bytes 1065984 | tf_op jit(solution)/shard_map/qd,kd->qk/dot_general | solution.py:78
  80.0 2.2 %fusion.106 = (f32[256]{0:T(256)S(1)}, f32[256,896]{1,0:T(8,128)}) fusion(bf16[896,8,64]{0,2,1:T(8,128)(2,1)} %bitcast.338, bf16[256,1,64]{0,2,1:T(8,128)(2,1)S(1)} %copy.69), kind=kOutput, calls=%fused_computation.211 | convolution fusion | flops 29818624 | bytes 1065984 | tf_op jit(solution)/shard_map/qd,kd->qk/dot_general | solution.py:78
  82.3 2.1 %fusion.107 = (f32[256]{0:T(256)S(1)}, f32[256,896]{1,0:T(8,128)}) fusion(bf16[896,8,64]{0,2,1:T(8,128)(2,1)} %bitcast.339, bf16[256,1,64]{0,2,1:T(8,128)(2,1)S(1)} %copy.70), kind=kOutput, calls=%fused_computation.212 | convolution fusion | flops 29818624 | bytes 1065984 | tf_op jit(solution)/shard_map/qd,kd->qk/dot_general | solution.py:78
  84.6 0.7 reshape.483
  85.3 3.9 %all-to-all-start.3 = ((f32[8,1,256]{2,1,0:T(1,128)}), f32[8,1,256]{2,1,0:T(1,128)S(1)}, u32[]{:S(2)}, u32[]{:S(2)}) async-start(f32[8,1,256]{2,1,0:T(1,128)} %reshape.483), calls=%async_computation.3 | async-start | bytes 16384 | tf_op jit(solution)/shard_map/all_to_all | solution.py:105
  94.9 1.0 copy-done.14
  96.7 0.7 reshape.485
  97.3 4.2 %all-to-all-start.4 = ((f32[8,1,256]{2,1,0:T(1,128)}), f32[8,1,256]{2,1,0:T(1,128)S(1)}, u32[]{:S(2)}, u32[]{:S(2)}) async-start(f32[8,1,256]{2,1,0:T(1,128)} %reshape.485), calls=%async_computation.4 | async-start | bytes 16384 | tf_op jit(solution)/shard_map/all_to_all | solution.py:106
  101.6 0.9 fusion.17
  102.5 1.3 copy.79
  103.8 1.5 reshape.481
  105.3 4.4 %all-to-all-start.2 = ((f32[8,1,16384]{2,1,0:T(1,128)}), f32[8,1,16384]{2,1,0:T(1,128)S(1)}, u32[]{:S(2)}, u32[]{:S(2)}) async-start(f32[8,1,16384]{2,1,0:T(1,128)} %reshape.481), calls=%async_computation.2 | async-start | bytes 1048576 | tf_op jit(solution)/shard_map/all_to_all | solution.py:107
  109.7 1.0 fusion.2
  110.6 1.7 %fusion.25 = bf16[896,8,64]{0,2,1:T(8,128)(2,1)S(1)} fusion(f32[8,896,64]{1,2,0:T(8,128)} %fusion.2, f32[8,896]{1,0:T(8,128)S(1)} %copy-done.16), kind=kLoop, calls=%fused_computation.78 | loop fusion | flops 917504 | bytes 2781184 | tf_op jit(solution)/shard_map/convert_element_type | solution.py:64
  112.3 0.9 convert_element_type.94
  113.2 1.4 copy.59
  114.6 3.4 %all-to-all-done.2 = f32[8,1,16384]{2,1,0:T(1,128)S(1)} async-done(((f32[8,1,16384]{2,1,0:T(1,128)}), f32[8,1,16384]{2,1,0:T(1,128)S(1)}, u32[]{:S(2)}, u32[]{:S(2)}) %all-to-all-start.2) | async-done | bytes 524320 | tf_op jit(solution)/shard_map/all_to_all | solution.py:107
  118.0 4.9 %all-to-all-start = ((bf16[4,224,512]{2,1,0:T(8,128)(2,1)}), bf16[4,224,512]{2,1,0:T(8,128)(2,1)S(1)}, u32[]{:S(2)}, u32[]{:S(2)}) async-start(bf16[4,224,512]{2,1,0:T(8,128)(2,1)} %copy.59), calls=%async_computation | async-start | bytes 1835008 | tf_op jit(solution)/shard_map/all_to_all | solution.py:67
  123.3 0.7 reduce.3
  124.1 0.7 reduce.4
  124.9 1.9 %reduce.5 = f32[8,16384]{1,0:T(8,128)S(1)} reduce(f32[8,1,16384]{2,1,0:T(1,128)S(1)} %all-to-all-done.2, f32[]{:T(128)} %broadcast.430), dimensions={1}, to_apply=%all_to_all.21.reduce_sub_computation | reduce | bytes 1048580 | tf_op jit(solution)/shard_map/all_to_all | solution.py:107
  127.7 0.7 convert_element_type.110
  128.4 17.6 %all-to-all-done = bf16[4,224,512]{2,1,0:T(8,128)(2,1)S(1)} async-done(((bf16[4,224,512]{2,1,0:T(8,128)(2,1)}), bf16[4,224,512]{2,1,0:T(8,128)(2,1)S(1)}, u32[]{:S(2)}, u32[]{:S(2)}) %all-to-all-start) | async-done | bytes 917536 | tf_op jit(solution)/shard_map/all_to_all | solution.py:67
  146.2 1.2 copy.60
  147.4 0.7 copy.77
  148.4 1.2 multiply_convert_fusion
  (143 shorter events, 12.5 us)
Async XLA Ops:
  0.6 15.2 %copy-start.15 = (bf16[896,512]{1,0:T(8,128)(2,1)S(1)}, bf16[896,512]{1,0:T(8,128)(2,1)}, u32[]{:S(2)}) copy-start(bf16[896,512]{1,0:T(8,128)(2,1)} %param.7) | copy-start | bytes 2752516
  2.2 54.3 %all-to-all-start.1 = ((bf16[8,32,512]{2,1,0:T(8,128)(2,1)}), bf16[8,32,512]{2,1,0:T(8,128)(2,1)S(1)}, u32[]{:S(2)}, u32[]{:S(2)}) async-start(bf16[8,32,512]{2,1,0:T(8,128)(2,1)} %stack.124), calls=%async_computation.1 | async-start | bytes 524288 | tf_op jit(solution)/shard_map/all_to_all | solution.py:11
  16.5 8.1 %copy-start.6 = (bf16[896,512]{0,1:T(8,128)(2,1)}, bf16[896,512]{0,1:T(8,128)(2,1)S(1)}, u32[]{:S(2)}) copy-start(bf16[896,512]{0,1:T(8,128)(2,1)S(1)} %copy.56) | copy-start | bytes 2752516
  16.8 9.4 %copy-start.5 = (f32[896,256]{0,1:T(8,128)}, f32[896,256]{0,1:T(8,128)S(1)}, u32[]{:S(2)}) copy-start(f32[896,256]{0,1:T(8,128)S(1)} %get-tuple-element.45) | copy-start | bytes 2752516
  24.3 2.7 %copy-start.20 = (bf16[32,512]{1,0:T(8,128)(2,1)S(1)}, bf16[32,512]{1,0:T(8,128)(2,1)}, u32[]{:S(2)}) copy-start(bf16[32,512]{1,0:T(8,128)(2,1)} %param.12) | copy-start | bytes 98308
  36.2 4.9 %copy-start.19 = (f32[896]{0:T(1024)S(1)}, f32[896]{0:T(1024)}, u32[]{:S(2)}) copy-start(f32[896]{0:T(1024)} %get-tuple-element.48) | copy-start | bytes 10756
  36.2 4.9 %copy-start.18 = (f32[896]{0:T(1024)S(1)}, f32[896]{0:T(1024)}, u32[]{:S(2)}) copy-start(f32[896]{0:T(1024)} %get-tuple-element.50) | copy-start | bytes 10756
  36.2 4.9 %copy-start.2 = (f32[896,256]{0,1:T(8,128)S(1)}, f32[896,256]{0,1:T(8,128)}, u32[]{:S(2)}) copy-start(f32[896,256]{0,1:T(8,128)} %get-tuple-element.51) | copy-start | bytes 2752516
  36.2 5.1 %copy-start.17 = (f32[896]{0:T(1024)S(1)}, f32[896]{0:T(1024)}, u32[]{:S(2)}) copy-start(f32[896]{0:T(1024)} %get-tuple-element.52) | copy-start | bytes 10756
  36.2 5.1 %copy-start = (f32[896,256]{0,1:T(8,128)S(1)}, f32[896,256]{0,1:T(8,128)}, u32[]{:S(2)}) copy-start(f32[896,256]{0,1:T(8,128)} %get-tuple-element.53) | copy-start | bytes 2752516
  41.3 0.7 copy-start.24
  42.1 4.4 %copy-start.21 = (f32[896]{0:T(1024)S(1)}, f32[896]{0:T(1024)}, u32[]{:S(2)}) copy-start(f32[896]{0:T(1024)} %get-tuple-element.43) | copy-start | bytes 10756
  46.6 4.5 %copy-start.4 = (f32[896,256]{0,1:T(8,128)S(1)}, f32[896,256]{0,1:T(8,128)}, u32[]{:S(2)}) copy-start(f32[896,256]{0,1:T(8,128)} %get-tuple-element.49) | copy-start | bytes 2752516
  46.6 5.5 %copy-start.3 = (f32[896,256]{0,1:T(8,128)S(1)}, f32[896,256]{0,1:T(8,128)}, u32[]{:S(2)}) copy-start(f32[896,256]{0,1:T(8,128)} %get-tuple-element.51) | copy-start | bytes 2752516
  48.8 4.1 %copy-start.1 = (f32[896,256]{0,1:T(8,128)S(1)}, f32[896,256]{0,1:T(8,128)}, u32[]{:S(2)}) copy-start(f32[896,256]{0,1:T(8,128)} %get-tuple-element.53) | copy-start | bytes 2752516
  59.9 2.7 %copy-start.25 = (f32[256]{0:T(256)}, f32[256]{0:T(256)S(1)}, u32[]{:S(2)}) copy-start(f32[256]{0:T(256)S(1)} %get-tuple-element.60) | copy-start | bytes 3076
  77.5 7.1 %copy-start.22 = (f32[1,8,32]{2,0,1:T(1,128)S(1)}, f32[1,8,32]{2,0,1:T(1,128)}, u32[]{:S(2)}) copy-start(f32[1,8,32]{2,0,1:T(1,128)} %stack.128) | copy-start | bytes 3076
  77.5 7.1 %copy-start.23 = (f32[1,8,32]{2,0,1:T(1,128)S(1)}, f32[1,8,32]{2,0,1:T(1,128)}, u32[]{:S(2)}) copy-start(f32[1,8,32]{2,0,1:T(1,128)} %stack.129) | copy-start | bytes 3076
  77.6 11.7 %copy-start.26 = (f32[256]{0:T(256)S(1)}, f32[256]{0:T(256)}, u32[]{:S(2)}) copy-start(f32[256]{0:T(256)} %copy-done.25) | copy-start | bytes 3076
  79.9 9.6 %copy-start.27 = (f32[256]{0:T(256)S(1)}, f32[256]{0:T(256)}, u32[]{:S(2)}) copy-start(f32[256]{0:T(256)} %get-tuple-element.62) | copy-start | bytes 3076
  82.3 7.6 %copy-start.28 = (f32[256]{0:T(256)S(1)}, f32[256]{0:T(256)}, u32[]{:S(2)}) copy-start(f32[256]{0:T(256)} %get-tuple-element.64) | copy-start | bytes 3076
  85.3 12.1 %all-to-all-start.3 = ((f32[8,1,256]{2,1,0:T(1,128)}), f32[8,1,256]{2,1,0:T(1,128)S(1)}, u32[]{:S(2)}, u32[]{:S(2)}) async-start(f32[8,1,256]{2,1,0:T(1,128)} %reshape.483), calls=%async_computation.3 | async-start | bytes 16384 | tf_op jit(solution)/shard_map/all_to_all | solution.py:105
  89.2 1.2 copy-start.7
  89.2 1.5 copy-start.8
  89.3 1.5 copy-start.29
  89.6 1.5 copy-start.9
  90.4 1.3 copy-start.10
  90.7 1.3 copy-start.11
  91.1 1.3 copy-start.12
  91.7 1.3 copy-start.13
  94.9 1.0 copy-start.14
  97.3 7.9 %all-to-all-start.4 = ((f32[8,1,256]{2,1,0:T(1,128)}), f32[8,1,256]{2,1,0:T(1,128)S(1)}, u32[]{:S(2)}, u32[]{:S(2)}) async-start(f32[8,1,256]{2,1,0:T(1,128)} %reshape.485), calls=%async_computation.4 | async-start | bytes 16384 | tf_op jit(solution)/shard_map/all_to_all | solution.py:106
  103.8 6.8 %copy-start.16 = (f32[8,896]{1,0:T(8,128)S(1)}, f32[8,896]{1,0:T(8,128)}, u32[]{:S(2)}) copy-start(f32[8,896]{1,0:T(8,128)} %stack.123) | copy-start | bytes 86020
  105.3 12.7 %all-to-all-start.2 = ((f32[8,1,16384]{2,1,0:T(1,128)}), f32[8,1,16384]{2,1,0:T(1,128)S(1)}, u32[]{:S(2)}, u32[]{:S(2)}) async-start(f32[8,1,16384]{2,1,0:T(1,128)} %reshape.481), calls=%async_computation.2 | async-start | bytes 1048576 | tf_op jit(solution)/shard_map/all_to_all | solution.py:107
  118.0 28.0 %all-to-all-start = ((bf16[4,224,512]{2,1,0:T(8,128)(2,1)}), bf16[4,224,512]{2,1,0:T(8,128)(2,1)S(1)}, u32[]{:S(2)}, u32[]{:S(2)}) async-start(bf16[4,224,512]{2,1,0:T(8,128)(2,1)} %copy.59), calls=%async_computation | async-start | bytes 1835008 | tf_op jit(solution)/shard_map/all_to_all | solution.py:67
  147.4 1.0 copy-start.30
